TPU v7x, 128 devices: a whole 4x4x4 slice. The times are simulated.
128 devices in a mesh: tok: 8 (over x, core), voc: 16 (over z, y).
Axes of the slice: x: 4, y: 4, z: 4, core: 2. Of those that a mesh axis runs over, the one named last changes fastest.
Arguments:
- hidden: bfloat16 [256, 32, 2048], P(('tok', 'voc')), may hold values from -40 to 40
- norm_gain: float32 [2048], replicated, may hold values from 0.5 to 1.5
- head_weight: bfloat16 [2048, 102400], P(None, 'voc'), may hold values from -2 to 2
- lengths: int32 [256], P(('tok', 'voc')), may hold values from 12 to 24, as said below
- offsets: int32 [256], P(('tok', 'voc')), may hold values from 0 to 8
- slot_request: int32 [256], replicated, may hold values from 0 to 255, each once
- targets: int32 [256, 32], P(('tok', 'voc')), may hold values from 0 to 102399
Outputs:
- token_logprob: float32 [256, 32], P(('tok', 'voc'))
- token_entropy: float32 [256, 32], P(('tok', 'voc'))
Inputs may be any that keep to these rules, and one draw needn't show every extreme that they name: `lengths`: each request has 12 to 24 response rows; all 2 requests of some one scoring device have exactly 24. Response rows end within the window: offsets + lengths <= 32. `slot_request`: every request appears in exactly one slot.
All inputs are finite; a program needn't handle non-finite values.
Results may differ from a plain program's by a relative error of at most 0.00145.
Values may be sent and summed in bfloat16 or wider, within the bound.
A program may use at most 128 MiB of HBM per device.

v0:
```python
import jax
import jax.numpy as jnp
from jax import lax
from jax.sharding import PartitionSpec as P

EPS = 1e-06


def normalize(hidden, norm_gain):
    values = hidden.astype(jnp.float32)
    square = jnp.mean(values * values, axis=-1, keepdims=True)
    return (values * lax.rsqrt(square + EPS) * norm_gain).astype(jnp.bfloat16)


def shards(hidden, norm_gain, head_weight, lengths, offsets, slot_request, targets):
    req_dev, span, width = hidden.shape
    vocab_dev = head_weight.shape[1]
    normed = normalize(hidden, norm_gain).reshape(req_dev * span, width)
    position = jnp.arange(span, dtype=jnp.int32)[None, :]
    in_span = (
        (position >= offsets[:, None]) & (position < offsets[:, None] + lengths[:, None])
    ).reshape(-1)
    flat_targets = targets.reshape(-1)
    own_count = normed.shape[0]
    group_matrix, group_targets = (
        lax.all_gather(normed, "voc", axis=0, tiled=True),
        lax.all_gather(flat_targets, "voc", axis=0, tiled=True),
    )
    logits = jnp.dot(group_matrix, head_weight, preferred_element_type=jnp.float32)
    shard_index = lax.axis_index("voc")
    local_column = group_targets - shard_index * vocab_dev
    target_hit = jnp.arange(vocab_dev, dtype=jnp.int32)[None, :] == local_column[:, None]
    picked = jnp.sum(jnp.where(target_hit, logits, 0.0), axis=1)
    row_peak = jnp.max(logits, axis=1)
    scaled = jnp.exp(logits - row_peak[:, None])
    exp_sum = jnp.sum(scaled, axis=1)
    exp_dot = jnp.sum(scaled * logits, axis=1)
    first_row = shard_index * own_count
    peak_all = lax.pmax(row_peak, "voc")
    rescale = jnp.exp(row_peak - peak_all)
    sum_all, dot_all, pick_all = lax.psum((exp_sum * rescale, exp_dot * rescale, picked), "voc")
    peak_own = lax.dynamic_slice_in_dim(peak_all, first_row, own_count)
    sum_own = lax.dynamic_slice_in_dim(sum_all, first_row, own_count)
    dot_own = lax.dynamic_slice_in_dim(dot_all, first_row, own_count)
    pick_own = lax.dynamic_slice_in_dim(pick_all, first_row, own_count)
    log_total = jnp.log(sum_own)
    logprob = pick_own - peak_own - log_total
    entropy = peak_own + log_total - dot_own / sum_own
    logprob_rows = jnp.where(in_span, logprob, 0.0).reshape(req_dev, span)
    entropy_rows = jnp.where(in_span, entropy, 0.0).reshape(req_dev, span)
    device = lax.axis_index(("tok", "voc"))
    every_logprob, every_entropy = (
        lax.all_gather(logprob_rows, ("tok", "voc"), axis=0, tiled=True),
        lax.all_gather(entropy_rows, ("tok", "voc"), axis=0, tiled=True),
    )
    wanted = device * req_dev + jnp.arange(req_dev, dtype=jnp.int32)
    picking = slot_request[None, :] == wanted[:, None]
    token_logprob = jnp.sum(jnp.where(picking[:, :, None], every_logprob[None, :, :], 0.0), axis=1)
    token_entropy = jnp.sum(jnp.where(picking[:, :, None], every_entropy[None, :, :], 0.0), axis=1)
    return (token_logprob, token_entropy)


def solution(mesh):
    placed = (
        P(("tok", "voc"), None, None),
        P(),
        P(None, "voc"),
        P(("tok", "voc")),
        P(("tok", "voc")),
        P(),
        P(("tok", "voc"), None),
    )
    return jax.shard_map(
        shards,
        mesh=mesh,
        in_specs=placed,
        out_specs=(P(("tok", "voc"), None), P(("tok", "voc"), None)),
        check_vma=False,
    )
```

profile of v0, /device:TPU:1, one launch (start us, length us, event | category | flops | bytes accessed | tf_op | source)
XLA Modules:
  0.0 325.5 jit_solution(2216714420504681096)
XLA Ops:
  7.2 0.0 all-gather.4.cloned.1.call-start
  7.2 1.1 fusion.1
  8.3 1.8 fusion.3
  10.1 0.0 all-gather.4.cloned.1.call-update
  10.1 0.7 add.46
  10.8 0.7 compare_and_fusion
  11.5 0.1 and.10
  11.6 0.8 reshape.74
  12.4 1.2 dynamic-slice
  14.3 0.2 dynamic-update-slice
  14.5 14.8 %all-reduce = s32[1024]{0:T(1024)S(1)} all-reduce(s32[1024]{0:T(1024)S(1)} %dynamic-update-slice), channel_id=1, replica_groups=mesh['tok'=8,'voc'=16] {'voc'}, use_global_device_ids=true, to_apply=%add | all-reduce | flops 1024 | bytes 8192
  29.4 0.8 broadcast_compare_fusion
  30.1 34.7 %all-gather.4.cloned.1.call-done = bf16[1024,2048]{1,0:T(8,128)(2,1)} async-done(((bf16[64,2048]{1,0:T(8,128)(2,1)}), bf16[1024,2048]{1,0:T(8,128)(2,1)}) %all-gather.4.cloned.1.call-update) | async-done | bytes 4194320 | tf_op jit(solution)/shard_map/all_gather | solution.py:26
  64.8 34.9 %fusion.6 = (f32[1024]{0:T(1024)S(1)}, f32[1024,6400]{1,0:T(8,128)}) fusion(bf16[1024,2048]{1,0:T(8,128)(2,1)} %all-gather.4.cloned.1.call-done, bf16[2048,6400]{1,0:T(8,128)(2,1)} %param.9), kind=kOutput, calls=%fused_computation.22 | convolution fusion | flops 26850099200 | bytes 56627200 | tf_op jit(solution)/shard_map/dot_general | solution.py:29
  99.7 31.2 %pmax.7 = f32[1024]{0:T(1024)S(1)} all-reduce(f32[1024]{0:T(1024)S(1)} %get-tuple-element.14), channel_id=1, replica_groups=mesh['tok'=8,'voc'=16] {'voc'}, use_global_device_ids=true, to_apply=%region_4.5 | all-reduce | flops 1024 | bytes 8192 | tf_op jit(solution)/shard_map/pmax | solution.py:39
  131.0 11.4 %multiply_reduce_fusion = (f32[1024]{0:T(1024)S(1)}, f32[1024]{0:T(1024)S(1)}, f32[1024]{0:T(1024)S(1)}) fusion(f32[1024,6400]{1,0:T(8,128)} %get-tuple-element.15, f32[1024]{0:T(1024)S(1)} %get-tuple-element.14, s32[1024]{0:T(1024)S(1)} %broadcast_subtract_fusion), kind=kLoop, calls=%fused_computation | loop fusion | flops 45872128 | bytes 26234880 | tf_op jit(solution)/shard_map/reduce_sum | solution.py:37
  142.4 55.9 %all-reduce.1 = (f32[1024]{0:T(1024)S(1)}, f32[1024]{0:T(1024)S(1)}, f32[1024]{0:T(1024)S(1)}) all-reduce(f32[1024]{0:T(1024)S(1)} %get-tuple-element.13, f32[1024]{0:T(1024)S(1)} %get-tuple-element.12, f32[1024]{0:T(1024)S(1)} %get-tuple-element.4), channel_id=1, replica_groups=mesh['tok'=8,'voc'=16] {'voc'}, use_global_device_ids=true, to_apply=%region_9.10 | all-reduce | flops 3072 | bytes 24576 | tf_op jit(solution)/shard_map/psum | solution.py:41
  198.3 0.1 subtract_select_fusion.1
  198.4 0.1 reshape.79
  198.5 69.1 %all-gather.1 = f32[128,2,32]{2,1,0:T(2,128)S(1)} all-gather(f32[1,2,32]{2,1,0:T(2,128)S(1)} %reshape.79), channel_id=1, replica_groups=mesh['tok'=8,'voc'=16] {'tok','voc'}, dimensions={0}, use_global_device_ids=true | all-gather | bytes 33024 | tf_op jit(solution)/shard_map/all_gather | solution.py:54
  267.6 0.1 copy.10
  267.7 0.1 reshape.77
  267.7 50.2 %all-gather = f32[128,2,32]{2,1,0:T(2,128)S(1)} all-gather(f32[1,2,32]{2,1,0:T(2,128)S(1)} %reshape.77), channel_id=1, replica_groups=mesh['tok'=8,'voc'=16] {'tok','voc'}, dimensions={0}, use_global_device_ids=true | all-gather | bytes 33024 | tf_op jit(solution)/shard_map/all_gather | solution.py:53
  317.9 0.1 copy.9
  318.0 0.7 select_reduce_fusion.1
  (5 shorter events, 0.0 us)
Async XLA Ops:
  7.2 57.7 %all-gather.4.cloned.1.call-start = ((), (), s32[]{:S(2)}) async-start(), calls=%async_computation | async-start | bytes 4456448 | tf_op jit(solution)/shard_map/all_gather | solution.py:26
Sparse Core Ops, SparseCore 0:
  10.2 54.5 all-gather.3
where the time goes:
time: 327 us; the launch traced here: 326 us
  blocking collectives  221 us (68%)
  matrix products  34.9 us (11%)
  waiting for transfers between devices  34.7 us (11%)
  other arithmetic  17.2 us (5%)
  between operations  14.7 us (4%)
    all_gather x1, blocking collectives, shards(): lax.all_gather(entropy_rows, ('tok', 'voc'), axis=0, tiled=True)  69.1 us
    psum x1, blocking collectives, shards(): lax.psum((exp_sum * rescale, exp_dot * rescale, picked), 'voc')  55.9 us
    all_gather x1, blocking collectives, shards(): lax.all_gather(logprob_rows, ('tok', 'voc'), axis=0, tiled=True)  50.2 us
    dot_general x1, matrix products, shards(): jnp.dot(group_matrix, head_weight, preferred_element_type=jnp.float32)  34.9 us
    all_gather x1, waiting for transfers between devices, shards(): lax.all_gather(normed, 'voc', axis=0, tiled=True)  34.7 us
    pmax x1, blocking collectives, shards(): peak_all = lax.pmax(row_peak, 'voc')  31.2 us
    unnamed x1, blocking collectives  14.8 us
    reduce_sum x1, other arithmetic, shards(): exp_dot = jnp.sum(scaled * logits, axis=1)  11.4 us
  transfers between devices with their start and end apart: 1, of which 1 were waited for; matrix products, arithmetic and copies ran while one was open for 1% of the time, Pallas kernels for 0%

commit v1 on v0

v1 whole, which is shorter than its diff:
```python
import functools

import jax
import jax.numpy as jnp
from jax import lax
from jax.experimental import pallas as pl
from jax.experimental.pallas import tpu as pltpu
from jax.sharding import PartitionSpec as P

EPS = 1e-06
LIVE = 24
SIDE = 4
LOW = -1e30
MESH = pl.DeviceIdType.MESH


def kernel(
    n_tok, columns,
    hidden_ref, gain_ref, targets_ref, lengths_ref, offsets_ref, request_ref, weight_hbm,
    logprob_ref, entropy_ref,
    normed_ref, rows_ref, meta_ref, weight_ref, even_ref, odd_ref,
    peak_ref, sum_ref, dot_ref, pick_ref, goal_ref,
    stat_ref, every_ref, code_ref, final_ref, owner_ref,
    weight_sem, row_send, row_recv, meta_send, meta_recv,
    stat_send, stat_recv, owner_send, owner_recv, final_send, final_recv,
):
    req_dev, span, width = hidden_ref.shape
    vocab_dev = weight_hbm.shape[1]
    chunks = vocab_dev // columns
    shard_rows = req_dev * LIVE
    tok, voc = lax.axis_index("tok"), lax.axis_index("voc")
    core = lax.rem(tok, 2)
    high, low = voc // SIDE, lax.rem(voc, SIDE)
    a = low + core * (high - low)
    b = high + core * (low - high)

    def shard_of(b_at, a_at):
        high_at = b_at + core * (a_at - b_at)
        low_at = a_at + core * (b_at - a_at)
        return high_at * SIDE + low_at

    def ring(place, step):
        return lax.rem(place + step + SIDE, SIDE)

    a_next, a_prev, a_far = ring(a, 1), ring(a, -1), ring(a, 2)
    b_next, b_prev, b_far = ring(b, 1), ring(b, -1), ring(b, 2)
    mine = b * SIDE + a

    weight_copies = [
        pltpu.make_async_copy(weight_hbm.at[:, pl.ds(c * columns, columns)], weight_ref.at[c], weight_sem.at[c])
        for c in range(chunks)
    ]
    for copy in weight_copies:
        copy.start()

    barrier = pltpu.get_barrier_semaphore()
    to_a_next, to_a_prev = (tok, shard_of(b, a_next)), (tok, shard_of(b, a_prev))
    to_b_next, to_b_prev = (tok, shard_of(b_next, a)), (tok, shard_of(b_prev, a))
    for peer in (to_a_next, to_a_prev, to_b_next, to_b_prev):
        pl.semaphore_signal(barrier, inc=1, device_id=peer, device_id_type=MESH)
    for step in range(1, n_tok):
        pl.semaphore_signal(barrier, inc=1, device_id=(lax.rem(tok + step, n_tok), voc), device_id_type=MESH)

    lane = lax.broadcasted_iota(jnp.int32, (1, 128), 1)
    which = lax.rem(lane // span, req_dev)
    own_half = lane // (req_dev * span) == lax.rem(a, 2)
    offset = jnp.where(which == 0, offsets_ref[0], offsets_ref[1])
    length = jnp.where(which == 0, lengths_ref[0], lengths_ref[1])
    relative = lax.rem(lane, span) - offset
    alive = own_half & (relative >= 0) & (relative < length)
    code = jnp.where(alive, (lane // span) * span + relative + 1, 0)
    first_slot = (tok * SIDE * SIDE + voc) * req_dev
    request = jnp.where(own_half, jnp.where(which == 0, request_ref[first_slot], request_ref[first_slot + 1]), 0)
    goals = targets_ref[...]
    goals = jnp.concatenate([goals[0:1], goals[1:2], goals[0:1], goals[1:2]], axis=1)
    goals = jnp.where(own_half, goals, 0)
    meta_ref[b, a] = jnp.concatenate(
        [goals.astype(jnp.float32), code.astype(jnp.float32), request.astype(jnp.float32), jnp.zeros((5, 128), jnp.float32)], axis=0
    )

    for j in range(req_dev):
        values = hidden_ref[j].astype(jnp.float32)
        square = jnp.mean(values * values, axis=-1, keepdims=True)
        normed_ref[pl.ds(j * span, span), :] = (values * lax.rsqrt(square + EPS) * gain_ref[...]).astype(jnp.bfloat16)
    row = lax.broadcasted_iota(jnp.int32, (shard_rows, req_dev * span), 0)
    column = lax.broadcasted_iota(jnp.int32, (shard_rows, req_dev * span), 1)
    source = jnp.where(row < LIVE, row + offsets_ref[0], row - LIVE + span + offsets_ref[1])
    chosen = jnp.where(source == column, 1.0, 0.0).astype(jnp.bfloat16)
    own_rows = pl.ds(pl.multiple_of(a * shard_rows, shard_rows), shard_rows)
    rows_ref[b, own_rows, :] = jnp.dot(chosen, normed_ref[...], preferred_element_type=jnp.float32).astype(jnp.bfloat16)

    pl.semaphore_wait(barrier, 4 + n_tok - 1)

    def send(ref, index, sems, place, peer):
        copy = pltpu.make_async_remote_copy(
            src_ref=ref.at[index], dst_ref=ref.at[index], send_sem=sems[0].at[place], recv_sem=sems[1].at[place],
            device_id=peer, device_id_type=MESH,
        )
        copy.start()
        return copy

    row_sems, meta_sems = (row_send, row_recv), (meta_send, meta_recv)
    whole, left, right = pl.ds(0, width), pl.ds(0, width // 2), pl.ds(width // 2, width // 2)

    def rows_at(b_at, a_at, part):
        return (b_at, pl.ds(pl.multiple_of(a_at * shard_rows, shard_rows), shard_rows), part)

    def landed(ref, index, sems, place):
        pltpu.make_async_copy(ref.at[index], ref.at[index], sems[1].at[place]).wait()

    sends = []
    sends.append(send(rows_ref, rows_at(b, a, whole), row_sems, 0, to_a_next))
    sends.append(send(rows_ref, rows_at(b, a, whole), row_sems, 1, to_a_prev))
    sends.append(send(meta_ref, (b, a), meta_sems, 0, to_a_next))
    sends.append(send(meta_ref, (b, a), meta_sems, 1, to_a_prev))
    landed(rows_ref, rows_at(b, a_prev, whole), row_sems, 0)
    sends.append(send(rows_ref, rows_at(b, a_prev, left), row_sems, 2, to_a_next))
    landed(meta_ref, (b, a_prev), meta_sems, 0)
    sends.append(send(meta_ref, (b, a_prev), meta_sems, 2, to_a_next))
    landed(rows_ref, rows_at(b, a_next, whole), row_sems, 1)
    sends.append(send(rows_ref, rows_at(b, a_next, right), row_sems, 3, to_a_prev))
    landed(meta_ref, (b, a_next), meta_sems, 1)
    for k, a_at in enumerate((a, a_prev, a_next)):
        sends.append(send(rows_ref, rows_at(b, a_at, whole), row_sems, 4 + 2 * k, to_b_next))
        sends.append(send(rows_ref, rows_at(b, a_at, whole), row_sems, 5 + 2 * k, to_b_prev))
    landed(rows_ref, rows_at(b, a_far, left), row_sems, 2)
    landed(rows_ref, rows_at(b, a_far, right), row_sems, 3)
    landed(meta_ref, (b, a_far), meta_sems, 2)
    sends.append(send(rows_ref, rows_at(b, a_far, whole), row_sems, 10, to_b_next))
    sends.append(send(rows_ref, rows_at(b, a_far, whole), row_sems, 11, to_b_prev))
    sends.append(send(meta_ref, (b,), meta_sems, 3, to_b_next))
    sends.append(send(meta_ref, (b,), meta_sems, 4, to_b_prev))

    lines = (b, b_next, b_prev, b_far)
    buffers = (even_ref, odd_ref)
    sub_row = lax.broadcasted_iota(jnp.int32, (128, 128), 0).astype(jnp.float32) + 1.0
    sub_lane = lax.broadcasted_iota(jnp.int32, (128, 128), 1)

    def begin(line):
        peak_ref[...] = jnp.full_like(peak_ref, LOW)
        sum_ref[...] = jnp.zeros_like(sum_ref)
        dot_ref[...] = jnp.zeros_like(dot_ref)
        pick_ref[...] = jnp.zeros_like(pick_ref)
        for half in range(2):
            both = meta_ref[line, 2 * half] + meta_ref[line, 2 * half + 1]
            goal = jnp.sum(jnp.where(both[1:2] == sub_row, both[0:1], 0.0), axis=1, keepdims=True)
            goal_ref[pl.ds(half * 128, 128), :] = goal.astype(jnp.int32) - voc * vocab_dev - sub_lane

    def multiply(line, chunk, buffer):
        buffer[...] = jnp.dot(rows_ref[line], weight_ref[chunk], preferred_element_type=jnp.float32)

    def collect(chunk, buffer):
        for group in range(SIDE * shard_rows // 8):
            request_at, part = group // 3, group % 3
            at = pl.ds(request_at * span + part * 8, 8)
            logits = [buffer[pl.ds(group * 8, 8), pl.ds(c * 128, 128)] for c in range(columns // 128)]
            peak = peak_ref[at]
            top = functools.reduce(jnp.maximum, logits, peak)
            rescale = jnp.exp(peak - top)
            exp_sum, exp_dot = sum_ref[at] * rescale, dot_ref[at] * rescale
            picked, goal = pick_ref[at], goal_ref[at]
            for c, logit in enumerate(logits):
                scaled = jnp.exp(logit - top)
                exp_sum = exp_sum + scaled
                exp_dot = exp_dot + scaled * logit
                picked = jnp.where(goal == chunk * columns + c * 128, logit, picked)
            peak_ref[at], sum_ref[at], dot_ref[at], pick_ref[at] = top, exp_sum, exp_dot, picked

    def finish(line):
        for half in range(2):
            at = pl.ds(half * 128, 128)
            peak = peak_ref[at].T
            top = jnp.max(peak, axis=0, keepdims=True)
            rescale = jnp.exp(peak - top)
            stat_ref[line, pl.ds(half, 1), :] = top
            stat_ref[line, pl.ds(2 + half, 1), :] = jnp.sum(sum_ref[at].T * rescale, axis=0, keepdims=True)
            stat_ref[line, pl.ds(4 + half, 1), :] = jnp.sum(dot_ref[at].T * rescale, axis=0, keepdims=True)
            stat_ref[line, pl.ds(6 + half, 1), :] = jnp.sum(pick_ref[at].T, axis=0, keepdims=True)
        every_ref[mine, line] = stat_ref[line]

    def spread(line):
        @pl.loop(1, SIDE * SIDE)
        def _(step):
            peer = lax.rem(mine + step, SIDE * SIDE)
            pltpu.make_async_remote_copy(
                src_ref=stat_ref.at[line], dst_ref=every_ref.at[mine, line], send_sem=stat_send.at[0], recv_sem=stat_recv.at[0],
                device_id=(tok, shard_of(peer // SIDE, lax.rem(peer, SIDE))), device_id_type=MESH,
            ).start()

    def spread_tok(ref, index, send_sem, recv_sem):
        copies = []
        for step in range(1, n_tok):
            copy = pltpu.make_async_remote_copy(
                src_ref=ref.at[index], dst_ref=ref.at[index], send_sem=send_sem.at[step], recv_sem=recv_sem.at[step],
                device_id=(lax.rem(tok + step, n_tok), voc), device_id_type=MESH,
            )
            copy.start()
            copies.append(copy)
        return copies

    def steps(position, first):
        line = lines[position]
        one, two = buffers[first], buffers[1 - first]

        @pl.loop(0, (chunks - 1) // 2)
        def _(pair):
            multiply(line, 2 * pair + 1, two)
            collect(2 * pair, one)
            multiply(line, 2 * pair + 2, one)
            collect(2 * pair + 1, two)

    for copy in weight_copies:
        copy.wait()
    begin(lines[0])
    multiply(lines[0], 0, buffers[0])
    for position in range(4):
        first = position % 2
        steps(position, first)
        if position == 0:
            for k, a_at in enumerate((a, a_prev, a_next, a_far)):
                landed(rows_ref, rows_at(b_prev, a_at, whole), row_sems, 4 + 2 * k)
                landed(rows_ref, rows_at(b_next, a_at, whole), row_sems, 5 + 2 * k)
            sends.append(send(rows_ref, (b_prev, slice(None), left), row_sems, 12, to_b_next))
            sends.append(send(rows_ref, (b_next, slice(None), right), row_sems, 13, to_b_prev))
            landed(meta_ref, (b_prev,), meta_sems, 3)
            landed(meta_ref, (b_next,), meta_sems, 4)
            sends.append(send(meta_ref, (b_prev,), meta_sems, 5, to_b_next))
        if position == 2:
            landed(rows_ref, (b_far, slice(None), left), row_sems, 12)
            landed(rows_ref, (b_far, slice(None), right), row_sems, 13)
            landed(meta_ref, (b_far,), meta_sems, 5)
        if position < 3:
            multiply(lines[position + 1], 0, buffers[1 - first])
        collect(chunks - 1, buffers[first])
        finish(lines[position])
        if position < 3:
            begin(lines[position + 1])
        if position == 2:
            for line in lines[:3]:
                spread(line)
            for line in range(SIDE):
                for half in range(2):
                    both = meta_ref[line, 2 * half] + meta_ref[line, 2 * half + 1]
                    code_ref[pl.ds(2 * line + half, 1), :] = both[1:2]
                    owner_ref[tok, pl.ds(2 * line + half, 1), :] = both[2:3]
            owner_copies = spread_tok(owner_ref, (tok,), owner_send, owner_recv)
    spread(lines[3])
    for copy in sends:
        copy.wait_send()
    for copy in owner_copies:
        copy.wait()
    others = every_ref.at[pl.ds(0, SIDE * SIDE - 1)]
    pltpu.make_async_copy(others, others, stat_recv.at[0]).wait()
    pltpu.make_async_copy(others, others, stat_send.at[0]).wait()

    peers = range(SIDE * SIDE)
    for line in range(SIDE):
        peaks = [every_ref[s, line, pl.ds(0, 2), :] for s in peers]
        top = functools.reduce(jnp.maximum, peaks)
        exp_sum = exp_dot = picked = jnp.zeros((2, 128), jnp.float32)
        for s in peers:
            rescale = jnp.exp(peaks[s] - top)
            exp_sum = exp_sum + every_ref[s, line, pl.ds(2, 2), :] * rescale
            exp_dot = exp_dot + every_ref[s, line, pl.ds(4, 2), :] * rescale
            picked = picked + every_ref[s, line, pl.ds(6, 2), :]
        log_total = jnp.log(exp_sum)
        final_ref[tok, 0, pl.ds(2 * line, 2), :] = picked - top - log_total
        final_ref[tok, 1, pl.ds(2 * line, 2), :] = top + log_total - exp_dot / exp_sum
    code = code_ref[...].astype(jnp.int32)
    shift = jnp.where(code > 0, lax.broadcasted_iota(jnp.int32, (8, 128), 1) + 1 - code, -1)
    for kind in range(2):
        score = final_ref[tok, kind]
        placed = jnp.zeros((8, 128), jnp.float32)
        for amount in range(span - LIVE + 1):
            moved = score if amount == 0 else pltpu.roll(score, amount, 1)
            placed = jnp.where(shift == amount, moved, placed)
        final_ref[tok, kind] = placed
    for copy in spread_tok(final_ref, (tok,), final_send, final_recv):
        copy.wait()
    for k in range(req_dev):
        wanted = ((tok * SIDE * SIDE + voc) * req_dev + k).astype(jnp.float32)
        for kind, out_ref in enumerate((logprob_ref, entropy_ref)):
            found = jnp.zeros((8, 128), jnp.float32)
            for t in range(n_tok):
                found = found + jnp.where(owner_ref[t] == wanted, final_ref[t, kind], 0.0)
            found = jnp.sum(found, axis=0, keepdims=True)
            out_ref[pl.ds(k, 1), :] = sum(found[:, part * span:(part + 1) * span] for part in range(128 // span))


def shards(n_tok, columns, hidden, norm_gain, head_weight, lengths, offsets, slot_request, targets):
    req_dev, span, width = hidden.shape
    vocab_dev = head_weight.shape[1]
    chunks = vocab_dev // columns
    line_rows = SIDE * req_dev * LIVE
    f32 = jnp.float32
    vmem, smem = pl.BlockSpec(memory_space=pltpu.VMEM), pl.BlockSpec(memory_space=pltpu.SMEM)
    dma = pltpu.SemaphoreType.DMA
    return pl.pallas_call(
        functools.partial(kernel, n_tok, columns),
        out_shape=(jax.ShapeDtypeStruct((req_dev, span), f32),) * 2,
        in_specs=[vmem, vmem, vmem, smem, smem, smem, pl.BlockSpec(memory_space=pl.ANY)],
        out_specs=(vmem, vmem),
        scratch_shapes=[
            pltpu.VMEM((req_dev * span, width), jnp.bfloat16),
            pltpu.VMEM((SIDE, line_rows, width), jnp.bfloat16),
            pltpu.VMEM((SIDE, SIDE, 8, 128), f32),
            pltpu.VMEM((chunks, width, columns), jnp.bfloat16),
            pltpu.VMEM((line_rows, columns), f32),
            pltpu.VMEM((line_rows, columns), f32),
            pltpu.VMEM((256, 128), f32),
            pltpu.VMEM((256, 128), f32),
            pltpu.VMEM((256, 128), f32),
            pltpu.VMEM((256, 128), f32),
            pltpu.VMEM((256, 128), jnp.int32),
            pltpu.VMEM((SIDE, 8, 128), f32),
            pltpu.VMEM((SIDE * SIDE, SIDE, 8, 128), f32),
            pltpu.VMEM((8, 128), f32),
            pltpu.VMEM((n_tok, 2, 8, 128), f32),
            pltpu.VMEM((n_tok, 8, 128), f32),
            dma((chunks,)),
            dma((14,)), dma((14,)), dma((6,)), dma((6,)),
            dma((1,)), dma((1,)), dma((n_tok,)), dma((n_tok,)), dma((n_tok,)), dma((n_tok,)),
        ],
        compiler_params=pltpu.CompilerParams(
            collective_id=0, has_side_effects=True, vmem_limit_bytes=58 * 2**20
        ),
        name="score",
    )(hidden, norm_gain.reshape(1, width), targets, lengths, offsets, slot_request, head_weight)


def solution(mesh, columns=1280):
    placed = (
        P(("tok", "voc"), None, None),
        P(),
        P(None, "voc"),
        P(("tok", "voc")),
        P(("tok", "voc")),
        P(),
        P(("tok", "voc"), None),
    )
    return jax.shard_map(
        functools.partial(shards, mesh.shape["tok"], columns),
        mesh=mesh,
        in_specs=placed,
        out_specs=(P(("tok", "voc"), None), P(("tok", "voc"), None)),
        check_vma=False,
    )
```

time: 327 us -> 57.9 us (0.18)
  blocking collectives: 221 us -> 0 us
  Pallas kernels: 0 us -> 54.7 us
  matrix products: 34.9 us -> 0 us
  waiting for transfers between devices: 34.7 us -> 0 us
  other arithmetic: 17.2 us -> 0 us
  between operations: 14.7 us -> 0.64 us
    all_gather x2 -> x0, blocking collectives: 119 us -> none  [the longest x1 69.1 us: shards(): lax.all_gather(entropy_rows, ('tok', 'voc'), axis=0, tiled=True)]
    psum x1 -> x0, blocking collectives: 55.9 us -> none  [shards(): lax.psum((exp_sum * rescale, exp_dot * rescale, picked), 'voc')]
    pallas_call x0 -> x1, Pallas kernels: none -> 54.7 us  [shards(): pl.pallas_call(functools.partial(kernel, n_tok, columns), out_shape=(jax....]
    dot_general x1 -> x0, matrix products: 34.9 us -> none  [shards(): jnp.dot(group_matrix, head_weight, preferred_element_type=jnp.float32)]
    all_gather x1 -> x0, waiting for transfers between devices: 34.7 us -> none  [shards(): lax.all_gather(normed, 'voc', axis=0, tiled=True)]
    pmax x1 -> x0, blocking collectives: 31.2 us -> none  [shards(): peak_all = lax.pmax(row_peak, 'voc')]
    unnamed x1 -> x0, blocking collectives: 14.8 us -> none
    reduce_sum x3 -> x0, other arithmetic: 13.2 us -> none  [the longest x1 11.4 us: shards(): exp_dot = jnp.sum(scaled * logits, axis=1)]
  transfers between devices with their start and end apart: 1 -> 0, of which waited for: 1 -> 0; matrix products, arithmetic and copies ran while one was open for 1% -> 0% of each run, Pallas kernels for 0% -> 0%
where the time goes in v1:
time: 57.9 us; the launch traced here: 57.8 us
  Pallas kernels  54.7 us (94%)
  local copies, waits for them, and re-layouts  2.44 us (4%)
  between operations  0.64 us (1%)
    pallas_call x1, Pallas kernels, shards(): pl.pallas_call(functools.partial(kernel, n_tok, columns), out_shape=(jax....  54.7 us
    unnamed x2, local copies, waits for them, and re-layouts  2.44 us

profile of v1, /device:TPU:1, one launch (start us, length us, event | category | flops | bytes accessed | tf_op | source)
XLA Modules:
  0.0 57.8 jit_solution(9494296394497632702)
XLA Ops:
  0.6 54.7 %score.1 = (f32[2,32]{1,0:T(2,128)}, f32[2,32]{1,0:T(2,128)}) custom-call(bf16[2,32,2048]{2,1,0:T(8,128)(2,1)} %hidden_ref.1, f32[1,2048]{1,0:T(1,128)} %bitcast.1, s32[2,32]{1,0:T(2,128)} %targets_ref.1, s32[2]{0:T(128)} %lengths_ref.1, s32[2]{0:T(128)} %offsets_ref.1, s32[256]{0:T(256)} %request_ref.1, bf16[2048,6400]{1,0:T(8,128)(2,1)} %weight_hbm.1), custom_call_target="tpu_custom_call" | custom-call | tf_op jit(solution)/shard_map/score/pallas_call | solution.py:298
  55.4 1.2 %copy.11 = f32[2,32]{1,0:T(2,128)} copy(f32[2,32]{1,0:T(2,128)} %get-tuple-element.4) | data formatting | bytes 512
  56.6 1.2 %copy.12 = f32[2,32]{1,0:T(2,128)} copy(f32[2,32]{1,0:T(2,128)} %get-tuple-element.5) | data formatting | bytes 512

commit v2 on v1

v2 whole, which is shorter than its diff:
```python
import functools

import jax
import jax.numpy as jnp
from jax import lax
from jax.experimental import pallas as pl
from jax.experimental.pallas import tpu as pltpu
from jax.sharding import PartitionSpec as P

EPS = 1e-06
LIVE = 24
SIDE = 4
LOW = -1e30
MESH = pl.DeviceIdType.MESH


def kernel(
    n_tok, columns,
    hidden_ref, gain_ref, targets_ref, lengths_ref, offsets_ref, request_ref, weight_hbm,
    out_ref,
    normed_ref, rows_ref, meta_ref, weight_ref, even_ref, odd_ref,
    peak_ref, sum_ref, dot_ref, pick_ref, goal_ref,
    stat_ref, every_ref, code_ref, final_ref, owner_ref,
    weight_sem, row_send, row_recv, meta_send, meta_recv,
    stat_send, stat_recv, owner_send, owner_recv, final_send, final_recv,
):
    req_dev, span, width = hidden_ref.shape
    vocab_dev = weight_hbm.shape[1]
    chunks = vocab_dev // columns
    shard_rows = req_dev * LIVE
    tok, voc = lax.axis_index("tok"), lax.axis_index("voc")
    core = lax.rem(tok, 2)
    high, low = voc // SIDE, lax.rem(voc, SIDE)
    a = low + core * (high - low)
    b = high + core * (low - high)

    def shard_of(b_at, a_at):
        high_at = b_at + core * (a_at - b_at)
        low_at = a_at + core * (b_at - a_at)
        return high_at * SIDE + low_at

    def ring(place, step):
        return lax.rem(place + step + SIDE, SIDE)

    a_next, a_prev, a_far = ring(a, 1), ring(a, -1), ring(a, 2)
    b_next, b_prev, b_far = ring(b, 1), ring(b, -1), ring(b, 2)
    mine = b * SIDE + a

    weight_copies = [
        pltpu.make_async_copy(weight_hbm.at[:, pl.ds(c * columns, columns)], weight_ref.at[c], weight_sem.at[c])
        for c in range(chunks)
    ]
    for copy in weight_copies:
        copy.start()

    barrier = pltpu.get_barrier_semaphore()
    to_a_next, to_a_prev = (tok, shard_of(b, a_next)), (tok, shard_of(b, a_prev))
    to_b_next, to_b_prev = (tok, shard_of(b_next, a)), (tok, shard_of(b_prev, a))
    for peer in (to_a_next, to_a_prev, to_b_next, to_b_prev):
        pl.semaphore_signal(barrier, inc=1, device_id=peer, device_id_type=MESH)
    for step in range(1, n_tok):
        pl.semaphore_signal(barrier, inc=1, device_id=(lax.rem(tok + step, n_tok), voc), device_id_type=MESH)

    lane = lax.broadcasted_iota(jnp.int32, (1, 128), 1)
    which = lax.rem(lane // span, req_dev)
    own_half = lane // (req_dev * span) == lax.rem(a, 2)
    offset = jnp.where(which == 0, offsets_ref[0], offsets_ref[1])
    length = jnp.where(which == 0, lengths_ref[0], lengths_ref[1])
    relative = lax.rem(lane, span) - offset
    alive = own_half & (relative >= 0) & (relative < length)
    code = jnp.where(alive, (lane // span) * span + relative + 1, 0)
    first_slot = (tok * SIDE * SIDE + voc) * req_dev
    request = jnp.where(own_half, jnp.where(which == 0, request_ref[first_slot], request_ref[first_slot + 1]), 0)
    goals = targets_ref[...]
    goals = jnp.concatenate([goals[0:1], goals[1:2], goals[0:1], goals[1:2]], axis=1)
    goals = jnp.where(own_half, goals, 0)
    meta_ref[b, a] = jnp.concatenate(
        [goals.astype(jnp.float32), code.astype(jnp.float32), request.astype(jnp.float32), jnp.zeros((5, 128), jnp.float32)], axis=0
    )

    for j in range(req_dev):
        values = hidden_ref[j].astype(jnp.float32)
        square = jnp.mean(values * values, axis=-1, keepdims=True)
        normed_ref[pl.ds(j * span, span), :] = (values * lax.rsqrt(square + EPS) * gain_ref[...]).astype(jnp.bfloat16)
    row = lax.broadcasted_iota(jnp.int32, (shard_rows, req_dev * span), 0)
    column = lax.broadcasted_iota(jnp.int32, (shard_rows, req_dev * span), 1)
    source = jnp.where(row < LIVE, row + offsets_ref[0], row - LIVE + span + offsets_ref[1])
    chosen = jnp.where(source == column, 1.0, 0.0).astype(jnp.bfloat16)
    rows_ref[pl.ds(0, shard_rows), :] = jnp.dot(
        chosen, normed_ref[...], preferred_element_type=jnp.float32
    ).astype(jnp.bfloat16)
    peak_ref[...] = jnp.full_like(peak_ref, LOW)
    sum_ref[...] = jnp.zeros_like(sum_ref)
    dot_ref[...] = jnp.zeros_like(dot_ref)
    pick_ref[...] = jnp.zeros_like(pick_ref)

    line_rows = SIDE * shard_rows
    sub_row = lax.broadcasted_iota(jnp.int32, (128, 128), 0).astype(jnp.float32) + 1.0
    sub_lane = lax.broadcasted_iota(jnp.int32, (128, 128), 1)
    lines = (b, b_next, b_prev, b_far)
    a_order = (a, a_next, a_far, a_prev)
    buffers = (even_ref, odd_ref)
    blocks = ((0, shard_rows), (shard_rows, 3 * shard_rows), (line_rows, 2 * line_rows), (3 * line_rows, line_rows))
    sends = []

    def push(ref, source, target, sems, place, peer):
        copy = pltpu.make_async_remote_copy(
            src_ref=ref.at[source], dst_ref=ref.at[target], send_sem=sems[0].at[place], recv_sem=sems[1].at[place],
            device_id=peer, device_id_type=MESH,
        )
        copy.start()
        sends.append(copy)
        return copy

    def landed(ref, index, sems, place):
        pltpu.make_async_copy(ref.at[index], ref.at[index], sems[1].at[place]).wait()

    row_sems, meta_sems = (row_send, row_recv), (meta_send, meta_recv)
    whole, left, right = pl.ds(0, width), pl.ds(0, width // 2), pl.ds(width // 2, width // 2)

    def shard(line, place, part=whole):
        return (pl.ds(line * line_rows + place * shard_rows, shard_rows), part)

    def whole_line(line, part):
        return (pl.ds(line * line_rows, line_rows), part)

    def goals_of(position):
        line = lines[position]
        for half in range(2):
            both = meta_ref[line, 2 * half] + meta_ref[line, 2 * half + 1]
            goal = jnp.sum(jnp.where(both[1:2] == sub_row, both[0:1], 0.0), axis=1, keepdims=True)
            at = pl.ds(position * 256 + half * 128, 128)
            goal_ref[at, :] = goal.astype(jnp.int32) - voc * vocab_dev - sub_lane

    def own_goals():
        both = meta_ref[b, a]
        for half in range(2):
            goal = jnp.sum(jnp.where(both[1:2] == sub_row, both[0:1], 0.0), axis=1, keepdims=True)
            goal_ref[pl.ds(half * 128, 128), :] = goal.astype(jnp.int32) - voc * vocab_dev - sub_lane

    def multiply(block, chunk, buffer):
        start, count = blocks[block]
        buffer[pl.ds(0, count), :] = jnp.dot(
            rows_ref[pl.ds(start, count), :], weight_ref[chunk], preferred_element_type=jnp.float32
        )

    def collect(block, chunk, buffer):
        start, count = blocks[block]
        for group in range(count // 8):
            flat = start + group * 8
            position, place = flat // line_rows, flat % line_rows // shard_rows
            request_at, part = flat % shard_rows // LIVE, flat % LIVE
            base = position * 256 + request_at * span + part
            at = pl.ds(pl.multiple_of(a_order[place] * (req_dev * span) + base, 8), 8)
            logits = [buffer[pl.ds(group * 8, 8), pl.ds(c * 128, 128)] for c in range(columns // 128)]
            peak = peak_ref[at]
            top = functools.reduce(jnp.maximum, logits, peak)
            rescale = jnp.exp(peak - top)
            exp_sum, exp_dot = sum_ref[at] * rescale, dot_ref[at] * rescale
            picked, goal = pick_ref[at], goal_ref[at]
            for c, logit in enumerate(logits):
                scaled = jnp.exp(logit - top)
                exp_sum = exp_sum + scaled
                exp_dot = exp_dot + scaled * logit
                picked = jnp.where(goal == chunk * columns + c * 128, logit, picked)
            peak_ref[at], sum_ref[at], dot_ref[at], pick_ref[at] = top, exp_sum, exp_dot, picked

    def finish(position):
        for half in range(2):
            at = pl.ds(position * 256 + half * 128, 128)
            peak = peak_ref[at].T
            top = jnp.max(peak, axis=0, keepdims=True)
            rescale = jnp.exp(peak - top)
            stat_ref[position, pl.ds(half, 1), :] = top
            stat_ref[position, pl.ds(2 + half, 1), :] = jnp.sum(sum_ref[at].T * rescale, axis=0, keepdims=True)
            stat_ref[position, pl.ds(4 + half, 1), :] = jnp.sum(dot_ref[at].T * rescale, axis=0, keepdims=True)
            stat_ref[position, pl.ds(6 + half, 1), :] = jnp.sum(pick_ref[at].T, axis=0, keepdims=True)

    far_first = sorted(
        ((i, j) for i in range(SIDE) for j in range(SIDE) if i or j), key=lambda s: -(min(s[0], SIDE - s[0]) + min(s[1], SIDE - s[1]))
    )

    def spread(position):
        for i, j in far_first:
            pltpu.make_async_remote_copy(
                src_ref=stat_ref.at[position], dst_ref=every_ref.at[mine, lines[position]],
                send_sem=stat_send.at[0], recv_sem=stat_recv.at[0],
                device_id=(tok, shard_of(ring(b, i), ring(a, j))), device_id_type=MESH,
            ).start()
        every_ref[mine, lines[position]] = stat_ref[position]

    def spread_tok(ref, index, send_sem, recv_sem):
        copies = []
        for step in sorted(range(1, n_tok), key=lambda k: -min(k, n_tok - k)):
            copy = pltpu.make_async_remote_copy(
                src_ref=ref.at[index], dst_ref=ref.at[index], send_sem=send_sem.at[step], recv_sem=recv_sem.at[step],
                device_id=(lax.rem(tok + step, n_tok), voc), device_id_type=MESH,
            )
            copy.start()
            copies.append(copy)
        return copies

    def steps(block, first):
        one, two = buffers[first], buffers[1 - first]

        @pl.loop(0, (chunks - 1) // 2)
        def _(pair):
            multiply(block, 2 * pair + 1, two)
            collect(block, 2 * pair, one)
            multiply(block, 2 * pair + 2, one)
            collect(block, 2 * pair + 1, two)

    pl.semaphore_wait(barrier, 4 + n_tok - 1)
    own_next = push(rows_ref, shard(0, 0), shard(0, 3), row_sems, 0, to_a_next)
    own_prev = push(rows_ref, shard(0, 0), shard(0, 1), row_sems, 1, to_a_prev)
    push(meta_ref, (b, a), (b, a), meta_sems, 0, to_a_next)
    push(meta_ref, (b, a), (b, a), meta_sems, 1, to_a_prev)
    own_goals()

    for chunk in range(chunks):
        weight_copies[chunk].wait()
        multiply(0, chunk, buffers[chunk % 2])
        if chunk > 0:
            collect(0, chunk - 1, buffers[1 - chunk % 2])
        if chunk == min(1, chunks - 1):
            own_next.wait_send()
            own_prev.wait_send()
            push(rows_ref, shard(0, 0), shard(2, 0), row_sems, 4, to_b_next)
            push(rows_ref, shard(0, 0), shard(1, 0), row_sems, 5, to_b_prev)
        if chunk == min(2, chunks - 1):
            landed(rows_ref, shard(0, 3), row_sems, 0)
            push(rows_ref, shard(0, 3, left), shard(0, 2, left), row_sems, 2, to_a_next)
            landed(rows_ref, shard(0, 1), row_sems, 1)
            push(rows_ref, shard(0, 1, right), shard(0, 2, right), row_sems, 3, to_a_prev)
            landed(meta_ref, (b, a_prev), meta_sems, 0)
            push(meta_ref, (b, a_prev), (b, a_prev), meta_sems, 2, to_a_next)
            landed(meta_ref, (b, a_next), meta_sems, 1)
            for k, place in enumerate((1, 3)):
                push(rows_ref, shard(0, place), shard(2, place), row_sems, 6 + 2 * k, to_b_next)
                push(rows_ref, shard(0, place), shard(1, place), row_sems, 7 + 2 * k, to_b_prev)
    landed(rows_ref, shard(0, 2, left), row_sems, 2)
    landed(rows_ref, shard(0, 2, right), row_sems, 3)
    push(rows_ref, shard(0, 2), shard(2, 2), row_sems, 10, to_b_next)
    push(rows_ref, shard(0, 2), shard(1, 2), row_sems, 11, to_b_prev)
    landed(meta_ref, (b, a_far), meta_sems, 2)
    push(meta_ref, (b,), (b,), meta_sems, 3, to_b_next)
    push(meta_ref, (b,), (b,), meta_sems, 4, to_b_prev)

    at_chunk = (chunks - 1) % 2
    multiply(1, 0, buffers[1 - at_chunk])
    collect(0, chunks - 1, buffers[at_chunk])
    goals_of(0)
    first = 1 - at_chunk
    steps(1, first)
    for k, place in enumerate((0, 1, 3, 2)):
        landed(rows_ref, shard(2, place), row_sems, 4 + 2 * k)
        landed(rows_ref, shard(1, place), row_sems, 5 + 2 * k)
    push(rows_ref, whole_line(2, left), whole_line(3, left), row_sems, 12, to_b_next)
    push(rows_ref, whole_line(1, right), whole_line(3, right), row_sems, 13, to_b_prev)
    landed(meta_ref, (b_prev,), meta_sems, 3)
    landed(meta_ref, (b_next,), meta_sems, 4)
    push(meta_ref, (b_prev,), (b_prev,), meta_sems, 5, to_b_next)
    multiply(2, 0, buffers[1 - first])
    collect(1, chunks - 1, buffers[first])
    finish(0)
    goals_of(1)
    goals_of(2)
    first = 1 - first
    steps(2, first)
    landed(rows_ref, whole_line(3, left), row_sems, 12)
    landed(rows_ref, whole_line(3, right), row_sems, 13)
    landed(meta_ref, (b_far,), meta_sems, 5)
    multiply(3, 0, buffers[1 - first])
    collect(2, chunks - 1, buffers[first])
    goals_of(3)
    finish(1)
    finish(2)
    for position in range(3):
        spread(position)
    for line in range(SIDE):
        for half in range(2):
            both = meta_ref[line, 2 * half] + meta_ref[line, 2 * half + 1]
            code_ref[pl.ds(2 * line + half, 1), :] = both[1:2]
            owner_ref[tok, pl.ds(2 * line + half, 1), :] = both[2:3]
    owner_copies = spread_tok(owner_ref, (tok,), owner_send, owner_recv)
    first = 1 - first
    steps(3, first)
    collect(3, chunks - 1, buffers[first])
    finish(3)
    spread(3)
    for copy in sends:
        if copy is not own_next and copy is not own_prev:
            copy.wait_send()
    for copy in owner_copies:
        copy.wait()
    others = every_ref.at[pl.ds(0, SIDE * SIDE - 1)]
    pltpu.make_async_copy(others, others, stat_recv.at[0]).wait()
    pltpu.make_async_copy(others, others, stat_send.at[0]).wait()

    peers = range(SIDE * SIDE)
    for line in range(SIDE):
        peaks = [every_ref[s, line, pl.ds(0, 2), :] for s in peers]
        top = functools.reduce(jnp.maximum, peaks)
        exp_sum = exp_dot = picked = jnp.zeros((2, 128), jnp.float32)
        for s in peers:
            rescale = jnp.exp(peaks[s] - top)
            exp_sum = exp_sum + every_ref[s, line, pl.ds(2, 2), :] * rescale
            exp_dot = exp_dot + every_ref[s, line, pl.ds(4, 2), :] * rescale
            picked = picked + every_ref[s, line, pl.ds(6, 2), :]
        log_total = jnp.log(exp_sum)
        final_ref[tok, 0, pl.ds(2 * line, 2), :] = picked - top - log_total
        final_ref[tok, 1, pl.ds(2 * line, 2), :] = top + log_total - exp_dot / exp_sum
    code = code_ref[...].astype(jnp.int32)
    shift = jnp.where(code > 0, lax.broadcasted_iota(jnp.int32, (8, 128), 1) + 1 - code, -1)
    for kind in range(2):
        score = final_ref[tok, kind]
        placed = jnp.zeros((8, 128), jnp.float32)
        for amount in range(span - LIVE + 1):
            moved = score if amount == 0 else pltpu.roll(score, amount, 1)
            placed = jnp.where(shift == amount, moved, placed)
        final_ref[tok, kind] = placed
    for copy in spread_tok(final_ref, (tok,), final_send, final_recv):
        copy.wait()
    for k in range(req_dev):
        wanted = ((tok * SIDE * SIDE + voc) * req_dev + k).astype(jnp.float32)
        for kind in range(2):
            found = jnp.zeros((8, 128), jnp.float32)
            for t in range(n_tok):
                found = found + jnp.where(owner_ref[t] == wanted, final_ref[t, kind], 0.0)
            found = jnp.sum(found, axis=0, keepdims=True)
            out_ref[pl.ds(kind * req_dev + k, 1), :] = sum(found[:, part * span:(part + 1) * span] for part in range(128 // span))


def shards(n_tok, columns, hidden, norm_gain, head_weight, lengths, offsets, slot_request, targets):
    req_dev, span, width = hidden.shape
    vocab_dev = head_weight.shape[1]
    chunks = vocab_dev // columns
    line_rows = SIDE * req_dev * LIVE
    f32 = jnp.float32
    vmem, smem = pl.BlockSpec(memory_space=pltpu.VMEM), pl.BlockSpec(memory_space=pltpu.SMEM)
    dma = pltpu.SemaphoreType.DMA
    scores = pl.pallas_call(
        functools.partial(kernel, n_tok, columns),
        out_shape=jax.ShapeDtypeStruct((2 * req_dev, span), f32),
        in_specs=[vmem, vmem, vmem, smem, smem, smem, pl.BlockSpec(memory_space=pl.ANY)],
        out_specs=vmem,
        scratch_shapes=[
            pltpu.VMEM((req_dev * span, width), jnp.bfloat16),
            pltpu.VMEM((SIDE * line_rows, width), jnp.bfloat16),
            pltpu.VMEM((SIDE, SIDE, 8, 128), f32),
            pltpu.VMEM((chunks, width, columns), jnp.bfloat16),
            pltpu.VMEM((2 * line_rows, columns), f32),
            pltpu.VMEM((2 * line_rows, columns), f32),
            pltpu.VMEM((SIDE * 256, 128), f32),
            pltpu.VMEM((SIDE * 256, 128), f32),
            pltpu.VMEM((SIDE * 256, 128), f32),
            pltpu.VMEM((SIDE * 256, 128), f32),
            pltpu.VMEM((SIDE * 256, 128), jnp.int32),
            pltpu.VMEM((SIDE, 8, 128), f32),
            pltpu.VMEM((SIDE * SIDE, SIDE, 8, 128), f32),
            pltpu.VMEM((8, 128), f32),
            pltpu.VMEM((n_tok, 2, 8, 128), f32),
            pltpu.VMEM((n_tok, 8, 128), f32),
            dma((chunks,)),
            dma((14,)), dma((14,)), dma((6,)), dma((6,)),
            dma((1,)), dma((1,)), dma((n_tok,)), dma((n_tok,)), dma((n_tok,)), dma((n_tok,)),
        ],
        compiler_params=pltpu.CompilerParams(
            collective_id=0, has_side_effects=True, vmem_limit_bytes=58 * 2**20
        ),
        name="score",
    )(hidden, norm_gain.reshape(1, width), targets, lengths, offsets, slot_request, head_weight)
    return scores[:req_dev], scores[req_dev:]


def solution(mesh, columns=1280):
    placed = (
        P(("tok", "voc"), None, None),
        P(),
        P(None, "voc"),
        P(("tok", "voc")),
        P(("tok", "voc")),
        P(),
        P(("tok", "voc"), None),
    )
    return jax.shard_map(
        functools.partial(shards, mesh.shape["tok"], columns),
        mesh=mesh,
        in_specs=placed,
        out_specs=(P(("tok", "voc"), None), P(("tok", "voc"), None)),
        check_vma=False,
    )
```

time: 57.9 us -> 54.9 us (0.948)
  Pallas kernels: 54.7 us -> 52.8 us
  local copies, waits for them, and re-layouts: 2.44 us -> 1.32 us
    unnamed x2 -> x0, local copies, waits for them, and re-layouts: 2.44 us -> none
    pallas_call x1, Pallas kernels: 54.7 us -> 52.8 us  [shards(): pl.pallas_call(functools.partial(kernel, n_tok, columns), out_shape=jax.S...]
    slice x0 -> x1, local copies, waits for them, and re-layouts: none -> 1.32 us  [shards(): return (scores[:req_dev], scores[req_dev:])]
where the time goes in v2:
time: 54.9 us; the launch traced here: 54.8 us
  Pallas kernels  52.8 us (96%)
  local copies, waits for them, and re-layouts  1.32 us (2%)
  between operations  0.64 us (1%)
    pallas_call x1, Pallas kernels, shards(): pl.pallas_call(functools.partial(kernel, n_tok, columns), out_shape=jax.S...  52.8 us
    slice x1, local copies, waits for them, and re-layouts, shards(): return (scores[:req_dev], scores[req_dev:])  1.32 us

profile of v2, /device:TPU:1, one launch (start us, length us, event | category | flops | bytes accessed | tf_op | source)
XLA Modules:
  0.0 54.8 jit_solution(8088471329414766740)
XLA Ops:
  0.6 52.8 %score.1 = f32[4,32]{1,0:T(4,128)} custom-call(bf16[2,32,2048]{2,1,0:T(8,128)(2,1)} %hidden_ref.1, f32[1,2048]{1,0:T(1,128)} %bitcast.1, s32[2,32]{1,0:T(2,128)} %targets_ref.1, s32[2]{0:T(128)} %lengths_ref.1, s32[2]{0:T(128)} %offsets_ref.1, s32[256]{0:T(256)} %request_ref.1, bf16[2048,6400]{1,0:T(8,128)(2,1)} %weight_hbm.1), custom_call_target="tpu_custom_call" | custom-call | tf_op jit(solution)/shard_map/score/pallas_call | solution.py:342
  53.5 1.3 %fusion = (f32[2,32]{1,0:T(2,128)}, f32[2,32]{1,0:T(2,128)}) fusion(f32[4,32]{1,0:T(4,128)} %score.1), kind=kLoop, calls=%fused_computation | loop fusion | bytes 1024 | tf_op jit(solution)/shard_map/slice | solution.py:373

commit v3 on v2

--- a/solution.py
+++ b/solution.py
@@ -16,15 +16,16 @@
 
 def kernel(
     n_tok, columns,
-    hidden_ref, gain_ref, targets_ref, lengths_ref, offsets_ref, request_ref, weight_hbm,
+    hidden_hbm, gain_hbm, targets_hbm, lengths_hbm, offsets_hbm, request_hbm, weight_hbm,
     out_ref,
+    hidden_ref, gain_ref, targets_ref, lengths_ref, offsets_ref, request_ref, input_sem,
     normed_ref, rows_ref, meta_ref, weight_ref, even_ref, odd_ref,
     peak_ref, sum_ref, dot_ref, pick_ref, goal_ref,
     stat_ref, every_ref, code_ref, final_ref, owner_ref,
     weight_sem, row_send, row_recv, meta_send, meta_recv,
     stat_send, stat_recv, owner_send, owner_recv, final_send, final_recv,
 ):
-    req_dev, span, width = hidden_ref.shape
+    req_dev, span, width = hidden_hbm.shape
     vocab_dev = weight_hbm.shape[1]
     chunks = vocab_dev // columns
     shard_rows = req_dev * LIVE
@@ -46,11 +47,12 @@
     b_next, b_prev, b_far = ring(b, 1), ring(b, -1), ring(b, 2)
     mine = b * SIDE + a
 
-    weight_copies = [
-        pltpu.make_async_copy(weight_hbm.at[:, pl.ds(c * columns, columns)], weight_ref.at[c], weight_sem.at[c])
-        for c in range(chunks)
-    ]
-    for copy in weight_copies:
+    pairs = (
+        (hidden_hbm, hidden_ref), (gain_hbm, gain_ref), (targets_hbm, targets_ref),
+        (lengths_hbm, lengths_ref), (offsets_hbm, offsets_ref), (request_hbm, request_ref),
+    )
+    inputs = [pltpu.make_async_copy(src, dst, input_sem.at[n]) for n, (src, dst) in enumerate(pairs)]
+    for copy in inputs:
         copy.start()
 
     barrier = pltpu.get_barrier_semaphore()
@@ -60,6 +62,16 @@
         pl.semaphore_signal(barrier, inc=1, device_id=peer, device_id_type=MESH)
     for step in range(1, n_tok):
         pl.semaphore_signal(barrier, inc=1, device_id=(lax.rem(tok + step, n_tok), voc), device_id_type=MESH)
+
+    weight_copies = [
+        pltpu.make_async_copy(weight_hbm.at[:, pl.ds(c * columns, columns)], weight_ref.at[c], weight_sem.at[c])
+        for c in range(chunks)
+    ]
+    for copy in weight_copies:
+        copy.start()
+
+    for copy in inputs:
+        copy.wait()
 
     lane = lax.broadcasted_iota(jnp.int32, (1, 128), 1)
     which = lax.rem(lane // span, req_dev)
@@ -100,7 +112,11 @@
     lines = (b, b_next, b_prev, b_far)
     a_order = (a, a_next, a_far, a_prev)
     buffers = (even_ref, odd_ref)
-    blocks = ((0, shard_rows), (shard_rows, 3 * shard_rows), (line_rows, 2 * line_rows), (3 * line_rows, line_rows))
+    order = (
+        (0, 0), (0, 1), (0, 2), (0, 3), (1, 0), (1, 1), (2, 0), (2, 1),
+        (1, 3), (1, 2), (2, 3), (2, 2), (3, 0), (3, 1), (3, 3), (3, 2),
+    )
+    blocks = tuple((at * shard_rows, n * shard_rows) for at, n in ((0, 1), (1, 3), (4, 4), (8, 4), (12, 4)))
     sends = []
 
     def push(ref, source, target, sems, place, peer):
@@ -119,10 +135,10 @@
     whole, left, right = pl.ds(0, width), pl.ds(0, width // 2), pl.ds(width // 2, width // 2)
 
     def shard(line, place, part=whole):
-        return (pl.ds(line * line_rows + place * shard_rows, shard_rows), part)
-
-    def whole_line(line, part):
-        return (pl.ds(line * line_rows, line_rows), part)
+        return (pl.ds(order.index((line, place)) * shard_rows, shard_rows), part)
+
+    def couple(first, part):
+        return (pl.ds(first * shard_rows, 2 * shard_rows), part)
 
     def goals_of(position):
         line = lines[position]
@@ -148,7 +164,7 @@
         start, count = blocks[block]
         for group in range(count // 8):
             flat = start + group * 8
-            position, place = flat // line_rows, flat % line_rows // shard_rows
+            position, place = order[flat // shard_rows]
             request_at, part = flat % shard_rows // LIVE, flat % LIVE
             base = position * 256 + request_at * span + part
             at = pl.ds(pl.multiple_of(a_order[place] * (req_dev * span) + base, 8), 8)
@@ -252,11 +268,11 @@
     goals_of(0)
     first = 1 - at_chunk
     steps(1, first)
-    for k, place in enumerate((0, 1, 3, 2)):
+    for k, place in enumerate((0, 1)):
         landed(rows_ref, shard(2, place), row_sems, 4 + 2 * k)
         landed(rows_ref, shard(1, place), row_sems, 5 + 2 * k)
-    push(rows_ref, whole_line(2, left), whole_line(3, left), row_sems, 12, to_b_next)
-    push(rows_ref, whole_line(1, right), whole_line(3, right), row_sems, 13, to_b_prev)
+    push(rows_ref, couple(6, left), couple(12, left), row_sems, 12, to_b_next)
+    push(rows_ref, couple(4, right), couple(12, right), row_sems, 13, to_b_prev)
     landed(meta_ref, (b_prev,), meta_sems, 3)
     landed(meta_ref, (b_next,), meta_sems, 4)
     push(meta_ref, (b_prev,), (b_prev,), meta_sems, 5, to_b_next)
@@ -267,11 +283,21 @@
     goals_of(2)
     first = 1 - first
     steps(2, first)
-    landed(rows_ref, whole_line(3, left), row_sems, 12)
-    landed(rows_ref, whole_line(3, right), row_sems, 13)
-    landed(meta_ref, (b_far,), meta_sems, 5)
+    for k, place in enumerate((3, 2)):
+        landed(rows_ref, shard(2, place), row_sems, 8 + 2 * k)
+        landed(rows_ref, shard(1, place), row_sems, 9 + 2 * k)
+    push(rows_ref, couple(10, left), couple(14, left), row_sems, 14, to_b_next)
+    push(rows_ref, couple(8, right), couple(14, right), row_sems, 15, to_b_prev)
     multiply(3, 0, buffers[1 - first])
     collect(2, chunks - 1, buffers[first])
+    first = 1 - first
+    steps(3, first)
+    for k, at in enumerate((12, 14)):
+        landed(rows_ref, couple(at, left), row_sems, 12 + 2 * k)
+        landed(rows_ref, couple(at, right), row_sems, 13 + 2 * k)
+    landed(meta_ref, (b_far,), meta_sems, 5)
+    multiply(4, 0, buffers[1 - first])
+    collect(3, chunks - 1, buffers[first])
     goals_of(3)
     finish(1)
     finish(2)
@@ -284,8 +310,8 @@
             owner_ref[tok, pl.ds(2 * line + half, 1), :] = both[2:3]
     owner_copies = spread_tok(owner_ref, (tok,), owner_send, owner_recv)
     first = 1 - first
-    steps(3, first)
-    collect(3, chunks - 1, buffers[first])
+    steps(4, first)
+    collect(4, chunks - 1, buffers[first])
     finish(3)
     spread(3)
     for copy in sends:
@@ -337,20 +363,27 @@
     chunks = vocab_dev // columns
     line_rows = SIDE * req_dev * LIVE
     f32 = jnp.float32
-    vmem, smem = pl.BlockSpec(memory_space=pltpu.VMEM), pl.BlockSpec(memory_space=pltpu.SMEM)
+    vmem = pl.BlockSpec(memory_space=pltpu.VMEM)
     dma = pltpu.SemaphoreType.DMA
     scores = pl.pallas_call(
         functools.partial(kernel, n_tok, columns),
         out_shape=jax.ShapeDtypeStruct((2 * req_dev, span), f32),
-        in_specs=[vmem, vmem, vmem, smem, smem, smem, pl.BlockSpec(memory_space=pl.ANY)],
+        in_specs=[pl.BlockSpec(memory_space=pl.ANY)] * 7,
         out_specs=vmem,
         scratch_shapes=[
+            pltpu.VMEM(hidden.shape, hidden.dtype),
+            pltpu.VMEM((1, width), f32),
+            pltpu.VMEM(targets.shape, jnp.int32),
+            pltpu.SMEM(lengths.shape, jnp.int32),
+            pltpu.SMEM(offsets.shape, jnp.int32),
+            pltpu.SMEM(slot_request.shape, jnp.int32),
+            dma((6,)),
             pltpu.VMEM((req_dev * span, width), jnp.bfloat16),
             pltpu.VMEM((SIDE * line_rows, width), jnp.bfloat16),
             pltpu.VMEM((SIDE, SIDE, 8, 128), f32),
             pltpu.VMEM((chunks, width, columns), jnp.bfloat16),
-            pltpu.VMEM((2 * line_rows, columns), f32),
-            pltpu.VMEM((2 * line_rows, columns), f32),
+            pltpu.VMEM((line_rows, columns), f32),
+            pltpu.VMEM((line_rows, columns), f32),
             pltpu.VMEM((SIDE * 256, 128), f32),
             pltpu.VMEM((SIDE * 256, 128), f32),
             pltpu.VMEM((SIDE * 256, 128), f32),
@@ -362,7 +395,7 @@
             pltpu.VMEM((n_tok, 2, 8, 128), f32),
             pltpu.VMEM((n_tok, 8, 128), f32),
             dma((chunks,)),
-            dma((14,)), dma((14,)), dma((6,)), dma((6,)),
+            dma((16,)), dma((16,)), dma((6,)), dma((6,)),
             dma((1,)), dma((1,)), dma((n_tok,)), dma((n_tok,)), dma((n_tok,)), dma((n_tok,)),
         ],
         compiler_params=pltpu.CompilerParams(

time: 54.9 us -> 56.4 us (1.027)
  Pallas kernels: 52.8 us -> 54.3 us
    pallas_call x1, Pallas kernels: 52.8 us -> 54.3 us  [shards(): pl.pallas_call(functools.partial(kernel, n_tok, columns), out_shape=jax.S...]
where the time goes in v3:
time: 56.4 us; the launch traced here: 56.3 us
  Pallas kernels  54.3 us (96%)
  local copies, waits for them, and re-layouts  1.32 us (2%)
  between operations  0.64 us (1%)
    pallas_call x1, Pallas kernels, shards(): pl.pallas_call(functools.partial(kernel, n_tok, columns), out_shape=jax.S...  54.3 us
    slice x1, local copies, waits for them, and re-layouts, shards(): return (scores[:req_dev], scores[req_dev:])  1.32 us

profile of v3, /device:TPU:1, one launch (start us, length us, event | category | flops | bytes accessed | tf_op | source)
XLA Modules:
  0.0 56.3 jit_solution(6862307024225822081)
XLA Ops:
  0.6 54.3 %score.1 = f32[4,32]{1,0:T(4,128)} custom-call(bf16[2,32,2048]{2,1,0:T(8,128)(2,1)} %hidden_hbm.1, f32[1,2048]{1,0:T(1,128)} %bitcast.1, s32[2,32]{1,0:T(2,128)} %targets_hbm.1, s32[2]{0:T(128)} %lengths_hbm.1, s32[2]{0:T(128)} %offsets_hbm.1, s32[256]{0:T(256)} %request_hbm.1, bf16[2048,6400]{1,0:T(8,128)(2,1)} %weight_hbm.1), custom_call_target="tpu_custom_call" | custom-call | tf_op jit(solution)/shard_map/score/pallas_call | solution.py:368
  55.0 1.3 %fusion = (f32[2,32]{1,0:T(2,128)}, f32[2,32]{1,0:T(2,128)}) fusion(f32[4,32]{1,0:T(4,128)} %score.1), kind=kLoop, calls=%fused_computation | loop fusion | bytes 1024 | tf_op jit(solution)/shard_map/slice | solution.py:406

commit v4 on v2

--- a/solution.py
+++ b/solution.py
@@ -16,15 +16,16 @@
 
 def kernel(
     n_tok, columns,
-    hidden_ref, gain_ref, targets_ref, lengths_ref, offsets_ref, request_ref, weight_hbm,
+    hidden_hbm, gain_hbm, targets_hbm, lengths_hbm, offsets_hbm, request_hbm, weight_hbm,
     out_ref,
+    hidden_ref, gain_ref, targets_ref, lengths_ref, offsets_ref, request_ref, input_sem,
     normed_ref, rows_ref, meta_ref, weight_ref, even_ref, odd_ref,
     peak_ref, sum_ref, dot_ref, pick_ref, goal_ref,
     stat_ref, every_ref, code_ref, final_ref, owner_ref,
     weight_sem, row_send, row_recv, meta_send, meta_recv,
     stat_send, stat_recv, owner_send, owner_recv, final_send, final_recv,
 ):
-    req_dev, span, width = hidden_ref.shape
+    req_dev, span, width = hidden_hbm.shape
     vocab_dev = weight_hbm.shape[1]
     chunks = vocab_dev // columns
     shard_rows = req_dev * LIVE
@@ -46,11 +47,12 @@
     b_next, b_prev, b_far = ring(b, 1), ring(b, -1), ring(b, 2)
     mine = b * SIDE + a
 
-    weight_copies = [
-        pltpu.make_async_copy(weight_hbm.at[:, pl.ds(c * columns, columns)], weight_ref.at[c], weight_sem.at[c])
-        for c in range(chunks)
-    ]
-    for copy in weight_copies:
+    pairs = (
+        (hidden_hbm, hidden_ref), (gain_hbm, gain_ref), (targets_hbm, targets_ref),
+        (lengths_hbm, lengths_ref), (offsets_hbm, offsets_ref), (request_hbm, request_ref),
+    )
+    inputs = [pltpu.make_async_copy(src, dst, input_sem.at[n]) for n, (src, dst) in enumerate(pairs)]
+    for copy in inputs:
         copy.start()
 
     barrier = pltpu.get_barrier_semaphore()
@@ -60,6 +62,16 @@
         pl.semaphore_signal(barrier, inc=1, device_id=peer, device_id_type=MESH)
     for step in range(1, n_tok):
         pl.semaphore_signal(barrier, inc=1, device_id=(lax.rem(tok + step, n_tok), voc), device_id_type=MESH)
+
+    weight_copies = [
+        pltpu.make_async_copy(weight_hbm.at[:, pl.ds(c * columns, columns)], weight_ref.at[c], weight_sem.at[c])
+        for c in range(chunks)
+    ]
+    for copy in weight_copies:
+        copy.start()
+
+    for copy in inputs:
+        copy.wait()
 
     lane = lax.broadcasted_iota(jnp.int32, (1, 128), 1)
     which = lax.rem(lane // span, req_dev)
@@ -337,14 +349,21 @@
     chunks = vocab_dev // columns
     line_rows = SIDE * req_dev * LIVE
     f32 = jnp.float32
-    vmem, smem = pl.BlockSpec(memory_space=pltpu.VMEM), pl.BlockSpec(memory_space=pltpu.SMEM)
+    vmem = pl.BlockSpec(memory_space=pltpu.VMEM)
     dma = pltpu.SemaphoreType.DMA
     scores = pl.pallas_call(
         functools.partial(kernel, n_tok, columns),
         out_shape=jax.ShapeDtypeStruct((2 * req_dev, span), f32),
-        in_specs=[vmem, vmem, vmem, smem, smem, smem, pl.BlockSpec(memory_space=pl.ANY)],
+        in_specs=[pl.BlockSpec(memory_space=pl.ANY)] * 7,
         out_specs=vmem,
         scratch_shapes=[
+            pltpu.VMEM(hidden.shape, hidden.dtype),
+            pltpu.VMEM((1, width), f32),
+            pltpu.VMEM(targets.shape, jnp.int32),
+            pltpu.SMEM(lengths.shape, jnp.int32),
+            pltpu.SMEM(offsets.shape, jnp.int32),
+            pltpu.SMEM(slot_request.shape, jnp.int32),
+            dma((6,)),
             pltpu.VMEM((req_dev * span, width), jnp.bfloat16),
             pltpu.VMEM((SIDE * line_rows, width), jnp.bfloat16),
             pltpu.VMEM((SIDE, SIDE, 8, 128), f32),

time: 54.9 us -> 55.6 us (1.013)
  Pallas kernels: 52.8 us -> 53.5 us
    pallas_call x1, Pallas kernels: 52.8 us -> 53.5 us  [shards(): pl.pallas_call(functools.partial(kernel, n_tok, columns), out_shape=jax.S...]
where the time goes in v4:
time: 55.6 us; the launch traced here: 55.5 us
  Pallas kernels  53.5 us (96%)
  local copies, waits for them, and re-layouts  1.32 us (2%)
  between operations  0.64 us (1%)
    pallas_call x1, Pallas kernels, shards(): pl.pallas_call(functools.partial(kernel, n_tok, columns), out_shape=jax.S...  53.5 us
    slice x1, local copies, waits for them, and re-layouts, shards(): return (scores[:req_dev], scores[req_dev:])  1.32 us

profile of v4, /device:TPU:1, one launch (start us, length us, event | category | flops | bytes accessed | tf_op | source)
XLA Modules:
  0.0 55.5 jit_solution(8024980067392041637)
XLA Ops:
  0.6 53.5 %score.1 = f32[4,32]{1,0:T(4,128)} custom-call(bf16[2,32,2048]{2,1,0:T(8,128)(2,1)} %hidden_hbm.1, f32[1,2048]{1,0:T(1,128)} %bitcast.1, s32[2,32]{1,0:T(2,128)} %targets_hbm.1, s32[2]{0:T(128)} %lengths_hbm.1, s32[2]{0:T(128)} %offsets_hbm.1, s32[256]{0:T(256)} %request_hbm.1, bf16[2048,6400]{1,0:T(8,128)(2,1)} %weight_hbm.1), custom_call_target="tpu_custom_call" | custom-call | tf_op jit(solution)/shard_map/score/pallas_call | solution.py:354
  54.2 1.3 %fusion = (f32[2,32]{1,0:T(2,128)}, f32[2,32]{1,0:T(2,128)}) fusion(f32[4,32]{1,0:T(4,128)} %score.1), kind=kLoop, calls=%fused_computation | loop fusion | bytes 1024 | tf_op jit(solution)/shard_map/slice | solution.py:392
